TPU v7x, 512 devices: a whole 4x4x16 slice. The times are simulated.
512 devices in a mesh: section: 8 (over y_hi, x), head: 4 (over y_lo, core), tok: 16 (over z).
Axes of the slice: x: 4, y: 4 (y_hi: 2, y_lo: 2; y = y_hi * 2 + y_lo), z: 16, core: 2. Of those that a mesh axis runs over, the one named last changes fastest.
Arguments:
- held_cotangents: bfloat16 [8, 2, 2048, 2560], P('section', None, 'tok', 'head'), may hold values from -6 to 6
- entering_adjoint: bfloat16 [2048, 2560], P('tok', 'head'), may hold values from -6 to 6
- saved_queries: bfloat16 [8, 2048, 2560], P('section', 'tok', 'head'), may hold values from -1024 to 1024
- saved_keys: bfloat16 [8, 2048, 2560], P('section', 'tok', 'head'), may hold values from -20 to 20
- value_weight: bfloat16 [8, 2560, 2560], P('section', None, 'head'), may hold values from -0.125 to 0.125
- out_weight: bfloat16 [8, 2560, 2560], P('section', 'tok', 'head'), may hold values from -0.125 to 0.125
- block_gate: float32 [8, 2560], P('section'), may hold values from -3 to 3
- time_gate: float32 [32, 2560], replicated, may hold values from -3 to 3
- timestep: int32 [1], replicated, may hold values from 0 to 31
Outputs:
- passed: bfloat16 [8, 2, 2048, 2560], P('section', None, 'tok', 'head')
All inputs are finite; a program needn't handle non-finite values.
Results may differ from a plain program's by a relative error of at most 0.0085.
Values may be sent and summed in bfloat16 or wider, within the bound.
A program may use at most 64 MiB of HBM per device.

v0:
```python
import jax
import jax.numpy as jnp
from jax import lax
from jax.sharding import PartitionSpec as P

HD = 128
GUIDE = 3.0


def shifted(value, axis, steps):
    count = lax.axis_size(axis)
    leading, last = (max(0, -steps), min(count, count - steps))
    return lax.ppermute(value, axis, [(source, source + steps) for source in range(leading, last)])


def shards(
    held_cotangents,
    entering_adjoint,
    saved_queries,
    saved_keys,
    value_weight,
    out_weight,
    block_gate,
    time_gate,
    timestep,
):
    steps_index = jnp.arange(time_gate.shape[0])
    time_row = jnp.sum(
        jnp.where((steps_index == timestep[0])[:, None], time_gate, jnp.zeros_like(time_gate)),
        axis=0,
    )
    gate_row = block_gate[0] + time_row
    whole_cot = lax.all_gather(held_cotangents[0], "head", axis=2, tiled=True)
    scaled = (whole_cot.astype(jnp.float32) * gate_row).astype(jnp.bfloat16)
    out_full = lax.all_gather(out_weight[0], "tok", axis=0, tiled=True)
    attn_grad = jnp.einsum(
        "btd,dk->btk", scaled, out_full, preferred_element_type=jnp.float32
    ).astype(jnp.bfloat16)
    rows_here = saved_queries.shape[1]
    groups_here = saved_queries.shape[2] // HD
    score_scale = HD ** (-0.5)
    normal_grad = attn_grad[0]
    key_all = lax.all_gather(saved_keys[0], "tok", axis=0, tiled=True)
    key_heads = key_all.reshape(key_all.shape[0], groups_here, HD)
    query_heads = saved_queries[0].reshape(rows_here, groups_here, HD)
    scores = (
        jnp.einsum("ihe,jhe->hij", query_heads, key_heads, preferred_element_type=jnp.float32)
        * score_scale
    )
    row_top = jnp.max(scores, axis=2, keepdims=True)
    log_total = row_top + jnp.log(jnp.sum(jnp.exp(scores - row_top), axis=2, keepdims=True))
    weights = jnp.exp(scores - log_total).astype(jnp.bfloat16)
    grad_heads = normal_grad.reshape(rows_here, groups_here, HD)
    terms = jnp.einsum("hij,ihe->jhe", weights, grad_heads, preferred_element_type=jnp.float32)
    value_grad = lax.psum_scatter(
        terms.reshape(lax.axis_size("tok") * rows_here, groups_here * HD).astype(jnp.bfloat16),
        "tok",
        scatter_dimension=0,
        tiled=True,
    )
    stacked = jnp.stack([value_grad, attn_grad[1]])
    partial_back = jnp.einsum(
        "btk,dk->btd", stacked, value_weight[0], preferred_element_type=jnp.float32
    )
    back_sum = lax.psum_scatter(
        partial_back.astype(jnp.bfloat16), "head", scatter_dimension=2, tiled=True
    ).astype(jnp.float32)
    block_cot = (held_cotangents[0].astype(jnp.float32) + back_sum).astype(jnp.bfloat16)
    passed_on = shifted(block_cot, "section", -1)
    entering_full = entering_adjoint.astype(jnp.float32)
    fresh_rows = jnp.stack([(1.0 + GUIDE) * entering_full, -GUIDE * entering_full]).astype(
        jnp.bfloat16
    )
    is_last = lax.axis_index("section") == lax.axis_size("section") - 1
    return jnp.where(is_last, fresh_rows, passed_on)[None]


def solution(mesh):
    return jax.shard_map(
        shards,
        mesh=mesh,
        in_specs=(
            P("section", None, "tok", "head"),
            P("tok", "head"),
            P("section", "tok", "head"),
            P("section", "tok", "head"),
            P("section", None, "head"),
            P("section", "tok", "head"),
            P("section", None),
            P(),
            P(),
        ),
        out_specs=P("section", None, "tok", "head"),
        check_vma=False,
    )
```

profile of v0, /device:TPU:6, one launch (start us, length us, event | category | flops | bytes accessed | tf_op | source)
XLA Modules:
  0.0 357.0 jit_solution(16926532515218221262)
XLA Ops:
  6.5 0.0 copy-start
  6.5 0.0 all-gather.11.cloned.1.call-start
  6.5 1.9 copy.21
  8.4 0.0 all-gather.11.cloned.1.call-update
  8.4 0.0 all-gather.7.cloned.1.call-start
  8.5 0.7 all-gather.7.cloned.1.call-update
  9.2 0.0 all-gather.9.cloned.1.call-start
  9.2 0.7 all-gather.9.cloned.1.call-update
  9.9 0.0 reduce-scatter.5.cloned.1.call-start
  10.6 1.1 copy.20
  11.7 0.7 reduce
  12.4 1.1 select_reduce_fusion
  13.5 83.0 %all-gather.11.cloned.1.call-done = bf16[1,2048,640]{1,2,0:T(8,128)(2,1)} async-done(((bf16[1,128,640]{1,2,0:T(8,128)(2,1)}), bf16[1,2048,640]{1,2,0:T(8,128)(2,1)}) %all-gather.11.cloned.1.call-update) | async-done | bytes 2621456 | tf_op jit(solution)/shard_map/all_gather | solution.py:43
  96.6 2.7 multiply_reduce_fusion
  99.3 0.0 copy-start.1
  99.3 2.3 copy-done.1
  101.6 1.0 exponential_reduce_fusion
  102.6 21.9 %all-gather.7.cloned.1.call-done = bf16[1,2,128,2560]{3,2,1,0:T(8,128)(2,1)} async-done(((bf16[1,2,128,640]{3,2,1,0:T(8,128)(2,1)}), bf16[1,2,128,2560]{3,2,1,0:T(8,128)(2,1)}) %all-gather.7.cloned.1.call-update) | async-done | bytes 1310736 | tf_op jit(solution)/shard_map/all_gather | solution.py:33
  124.5 79.6 %all-gather.9.cloned.1.call-done = bf16[1,2560,640]{2,1,0:T(8,128)(2,1)} async-done(((bf16[1,160,640]{2,1,0:T(8,128)(2,1)}), bf16[1,2560,640]{2,1,0:T(8,128)(2,1)}) %all-gather.9.cloned.1.call-update) | async-done | bytes 3276816 | tf_op jit(solution)/shard_map/all_gather | solution.py:35
  204.2 3.5 fusion.9
  207.7 0.7 fusion.25
  208.4 0.8 copy.19
  209.2 5.3 %convolution_convert_fusion.1 = bf16[5,128,2048]{2,1,0:T(8,128)(2,1)} fusion(bf16[128,5,128]{0,2,1:T(8,128)(2,1)} %bitcast.51, f32[5,128,2048]{2,1,0:T(8,128)} %copy-done.1, f32[5,128]{1,0:T(8,128)S(1)} %log_add_fusion), kind=kOutput, calls=%fused_computation.7 | convolution fusion | flops 340787200 | bytes 8030720 | tf_op jit(solution)/shard_map/hij,ihe->jhe/dot_general | solution.py:54
  214.5 0.0 copy-start.2
  214.5 4.4 %copy.24 = bf16[2048,640]{1,0:T(8,128)(2,1)} copy(bf16[2048,640]{0,1:T(8,128)(2,1)} %bitcast.45) | data formatting | bytes 5242880 | tf_op jit(solution)/shard_map/convert_element_type | solution.py:56
  218.9 0.0 reduce-scatter.5.cloned.1.call-update
  218.9 0.0 reduce-scatter.7.cloned.1.call-start
  219.0 71.2 %reduce-scatter.5.cloned.1.call-done = bf16[128,640]{1,0:T(8,128)(2,1)} async-done(((bf16[2048,640]{1,0:T(8,128)(2,1)}), bf16[128,640]{1,0:T(8,128)(2,1)}) %reduce-scatter.5.cloned.1.call-update) | async-done | bytes 163856 | tf_op jit(solution)/shard_map/reduce_scatter | solution.py:55
  290.2 0.0 copy-done
  290.2 0.0 copy-done.2
  290.2 3.2 convolution_convert_fusion
  293.4 4.3 %copy.27 = bf16[2,128,2560]{1,0,2:T(2,128)(2,1)} copy(bf16[2,128,2560]{2,1,0:T(8,128)(2,1)} %convolution_convert_fusion) | data formatting | bytes 2621440
  297.7 0.0 copy-start.3
  297.7 2.6 copy.31
  300.3 0.0 reduce-scatter.7.cloned.1.call-update
  300.3 27.3 %reduce-scatter.7.cloned.1.call-done = bf16[640,256]{1,0:T(8,128)(2,1)} async-done(((bf16[2560,256]{1,0:T(8,128)(2,1)}), bf16[640,256]{1,0:T(8,128)(2,1)}) %reduce-scatter.7.cloned.1.call-update) | async-done | bytes 327696
  327.6 1.8 reshape.35
  329.4 1.9 copy.28
  331.3 1.9 fusion.14
  333.2 2.7 collective-permute-start
  336.0 0.0 copy-done.3
  336.0 12.7 %collective-permute-done = bf16[2,128,640]{2,1,0:T(8,128)(2,1)} collective-permute-done((bf16[2,128,640]{2,1,0:T(8,128)(2,1)}, bf16[2,128,640]{2,1,0:T(8,128)(2,1)}, u32[]{:S(2)}, u32[]{:S(2)}) %collective-permute-start) | collective-permute-done | bytes 327712 | tf_op jit(solution)/shard_map/ppermute | solution.py:13
  348.8 1.7 fusion.17
  (4 shorter events, 0.1 us)
Async XLA Ops:
  6.5 283.7 %copy-start = (bf16[1,2560,640]{2,1,0:T(8,128)(2,1)S(1)}, bf16[1,2560,640]{2,1,0:T(8,128)(2,1)}, u32[]{:S(2)}) copy-start(bf16[1,2560,640]{2,1,0:T(8,128)(2,1)} %param.13) | copy-start | bytes 9830404
  6.5 90.0 %all-gather.11.cloned.1.call-start = ((), (), s32[]{:S(2)}) async-start(), calls=%async_computation.5 | async-start | bytes 2785280 | tf_op jit(solution)/shard_map/all_gather | solution.py:43
  8.4 116.1 %all-gather.7.cloned.1.call-start = ((), (), s32[]{:S(2)}) async-start(), calls=%async_computation.3 | async-start | bytes 1638400 | tf_op jit(solution)/shard_map/all_gather | solution.py:33
  9.2 195.0 %all-gather.9.cloned.1.call-start = ((), (), s32[]{:S(2)}) async-start(), calls=%async_computation.4 | async-start | bytes 3481600 | tf_op jit(solution)/shard_map/all_gather | solution.py:35
  9.9 280.3 %reduce-scatter.5.cloned.1.call-start = ((), (), s32[]{:S(2)}) async-start(), calls=%async_computation.2 | async-start | bytes 2785280 | tf_op jit(solution)/shard_map/reduce_scatter | solution.py:55
  99.3 2.3 copy-start.1
  214.5 75.7 %copy-start.2 = (bf16[1,128,640]{2,1,0:T(8,128)(2,1)S(1)}, bf16[1,128,640]{2,1,0:T(8,128)(2,1)}, u32[]{:S(2)}) copy-start(bf16[1,128,640]{2,1,0:T(8,128)(2,1)} %get-tuple-element.6) | copy-start | bytes 491524
  218.9 108.7 %reduce-scatter.7.cloned.1.call-start = ((), (), s32[]{:S(2)}) async-start(), calls=%async_computation.6 | async-start | bytes 1638400
  297.7 38.3 %copy-start.3 = (bf16[128,640]{1,0:T(8,128)(2,1)S(1)}, bf16[128,640]{1,0:T(8,128)(2,1)}, u32[]{:S(2)}) copy-start(bf16[128,640]{1,0:T(8,128)(2,1)} %param.10) | copy-start | bytes 491524
  333.2 15.6 %collective-permute-start = (bf16[2,128,640]{2,1,0:T(8,128)(2,1)}, bf16[2,128,640]{2,1,0:T(8,128)(2,1)}, u32[]{:S(2)}, u32[]{:S(2)}) collective-permute-start(bf16[2,128,640]{2,1,0:T(8,128)(2,1)} %fusion.14), channel_id=1, source_target_pairs={{64,0},{128,64},{192,128},{256,192},{320,256},{384,320},{448,384},... | collective-permute-start | bytes 983048 | tf_op jit(solution)/shard_map/ppermute | solution.py:13
Sparse Core Ops, SparseCore 0:
  9.4 87.1 all-gather.10
  98.7 25.7 all-gather.6
  126.6 77.5 all-gather.8
  219.1 71.0 reduce-scatter.4
  300.4 27.1 reduce-scatter.6
where the time goes:
time: 358 us; the launch traced here: 357 us
  waiting for transfers between devices  297 us (83%)
  local copies, waits for them, and re-layouts  21.7 us (6%)
  matrix products  14.7 us (4%)
  between operations  13.9 us (4%)
  other arithmetic  6.49 us (2%)
    all_gather x1, waiting for transfers between devices, shards(): key_all = lax.all_gather(saved_keys[0], 'tok', axis=0, tiled=True)  83 us
    all_gather x1, waiting for transfers between devices, shards(): out_full = lax.all_gather(out_weight[0], 'tok', axis=0, tiled=True)  79.6 us
    reduce_scatter x1, waiting for transfers between devices, shards(): lax.psum_scatter(terms.reshape(lax.axis_size('tok') * rows_here, groups_h...  71.2 us
    unnamed x6, waiting for transfers between devices  28.7 us
    all_gather x1, waiting for transfers between devices, shards(): whole_cot = lax.all_gather(held_cotangents[0], 'head', axis=2, tiled=True)  21.9 us
    unnamed x14, local copies, waits for them, and re-layouts  15.8 us
    ppermute x1, waiting for transfers between devices, shifted(): lax.ppermute(value, axis, [(source, source + steps) for source in range(l...  12.7 us
  transfers between devices with their start and end apart: 6, of which 6 were waited for; matrix products, arithmetic and copies ran while one was open for 2% of the time, Pallas kernels for 0%

commit v1 on v0

--- a/solution.py
+++ b/solution.py
@@ -40,7 +40,9 @@
     groups_here = saved_queries.shape[2] // HD
     score_scale = HD ** (-0.5)
     normal_grad = attn_grad[0]
-    key_all = lax.all_gather(saved_keys[0], "tok", axis=0, tiled=True)
+    key_all = jnp.concatenate(
+        lax.all_to_all(jnp.stack([saved_keys[0]] * lax.axis_size("tok")), "tok", 0, 0), axis=0
+    )
     key_heads = key_all.reshape(key_all.shape[0], groups_here, HD)
     query_heads = saved_queries[0].reshape(rows_here, groups_here, HD)
     scores = (

time: 358 us -> 354 us (0.989)
  waiting for transfers between devices: 297 us -> 273 us
  starting transfers between devices: 2.91 us -> 18.3 us
  local copies, waits for them, and re-layouts: 21.7 us -> 30.7 us
    all_gather x1 -> x0, waiting for transfers between devices: 83 us -> none  [shards(): key_all = lax.all_gather(saved_keys[0], 'tok', axis=0, tiled=True)]
    all_gather x1, waiting for transfers between devices: 79.6 us -> 129 us  [shards(): out_full = lax.all_gather(out_weight[0], 'tok', axis=0, tiled=True)]
    all_to_all x0 -> x1, starting transfers between devices: none -> 15.4 us  [shards(): lax.all_to_all(jnp.stack([saved_keys[0]] * lax.axis_size('tok')), 'tok',...]
    another operation x0 -> x3, local copies, waits for them, and re-layouts: none -> 8.45 us  [the longest x1 5.22 us: shards(): key_heads = key_all.reshape(key_all.shape[0], groups_here, HD)]
    all_gather x1, waiting for transfers between devices: 21.9 us -> 30.3 us  [shards(): whole_cot = lax.all_gather(held_cotangents[0], 'head', axis=2, tiled=True)]
    all_to_all x0 -> x1, local copies, waits for them, and re-layouts: none -> 4.95 us  [shards(): lax.all_to_all(jnp.stack([saved_keys[0]] * lax.axis_size('tok')), 'tok',...]
    unnamed x14 -> x19, local copies, waits for them, and re-layouts: 15.8 us -> 11.4 us
    unnamed x6 -> x5, waiting for transfers between devices: 28.7 us -> 29 us
  transfers between devices with their start and end apart: 6 -> 6, of which waited for: 6 -> 5; matrix products, arithmetic and copies ran while one was open for 2% -> 2% of each run, Pallas kernels for 0% -> 0%
where the time goes in v1:
time: 354 us; the launch traced here: 353 us
  waiting for transfers between devices  273 us (77%)
  local copies, waits for them, and re-layouts  30.7 us (9%)
  starting transfers between devices  18.3 us (5%)
  between operations  13.9 us (4%)
  matrix products  12.2 us (3%)
  other arithmetic  5.78 us (2%)
    all_gather x1, waiting for transfers between devices, shards(): out_full = lax.all_gather(out_weight[0], 'tok', axis=0, tiled=True)  129 us
    reduce_scatter x1, waiting for transfers between devices, shards(): lax.psum_scatter(terms.reshape(lax.axis_size('tok') * rows_here, groups_h...  71.8 us
    all_gather x1, waiting for transfers between devices, shards(): whole_cot = lax.all_gather(held_cotangents[0], 'head', axis=2, tiled=True)  30.3 us
    unnamed x5, waiting for transfers between devices  29 us
    all_to_all x1, starting transfers between devices, shards(): lax.all_to_all(jnp.stack([saved_keys[0]] * lax.axis_size('tok')), 'tok',...  15.4 us
    ppermute x1, waiting for transfers between devices, shifted(): lax.ppermute(value, axis, [(source, source + steps) for source in range(l...  12.7 us
    unnamed x19, local copies, waits for them, and re-layouts  11.4 us
  transfers between devices with their start and end apart: 6, of which 5 were waited for; matrix products, arithmetic and copies ran while one was open for 2% of the time, Pallas kernels for 0%

profile of v1, /device:TPU:6, one launch (start us, length us, event | category | flops | bytes accessed | tf_op | source)
XLA Modules:
  0.0 353.5 jit_solution(10517423567697187382)
XLA Ops:
  6.5 0.0 copy-start
  6.5 1.2 copy.21
  7.8 2.0 stack.24
  9.8 0.0 copy-start.4
  9.8 0.0 copy-start.6
  9.8 15.4 %all-to-all-start = ((bf16[16,128,640]{1,2,0:T(8,128)(2,1)}), bf16[16,128,640]{1,2,0:T(8,128)(2,1)}, u32[]{:S(2)}, u32[]{:S(2)}) async-start(bf16[16,128,640]{1,2,0:T(8,128)(2,1)} %stack.24), calls=%async_computation | async-start | bytes 5242880 | tf_op jit(solution)/shard_map/all_to_all | solution.py:44
  25.2 0.0 all-gather.5.cloned.1.call-start
  25.2 0.7 all-gather.5.cloned.1.call-update
  25.9 0.0 all-gather.7.cloned.1.call-start
  25.9 0.7 all-gather.7.cloned.1.call-update
  26.6 0.0 reduce-scatter.5.cloned.1.call-start
  27.3 0.0 copy-done.4
  27.3 0.8 copy.20
  28.1 0.0 copy-done.6
  28.2 1.1 select_reduce_fusion
  29.3 30.3 %all-gather.5.cloned.1.call-done = bf16[1,2,128,2560]{3,2,1,0:T(8,128)(2,1)} async-done(((bf16[1,2,128,640]{3,2,1,0:T(8,128)(2,1)}), bf16[1,2,128,2560]{3,2,1,0:T(8,128)(2,1)}) %all-gather.5.cloned.1.call-update) | async-done | bytes 1310736 | tf_op jit(solution)/shard_map/all_gather | solution.py:33
  59.6 128.9 %all-gather.7.cloned.1.call-done = bf16[1,2560,640]{2,1,0:T(8,128)(2,1)} async-done(((bf16[1,160,640]{2,1,0:T(8,128)(2,1)}), bf16[1,2560,640]{2,1,0:T(8,128)(2,1)}) %all-gather.7.cloned.1.call-update) | async-done | bytes 3276816 | tf_op jit(solution)/shard_map/all_gather | solution.py:35
  188.5 3.5 fusion.9
  192.0 0.7 fusion.25
  192.7 0.8 copy.19
  193.5 0.0 all-to-all-done
  193.5 4.9 %copy.22 = bf16[16,128,640]{1,0,2:T(8,128)(2,1)} copy(bf16[16,128,640]{1,2,0:T(8,128)(2,1)} %all-to-all-done) | data formatting | bytes 5242880 | tf_op jit(solution)/shard_map/all_to_all | solution.py:44
  198.5 0.0 copy-start.1
  198.5 5.2 %reshape_reshape.3 = bf16[2048,5,128]{0,2,1:T(8,128)(2,1)} reshape(bf16[16,128,640]{1,0,2:T(8,128)(2,1)} %copy.22) | data formatting | bytes 5242880 | tf_op jit(solution)/shard_map/reshape;reshape | solution.py:46
  203.7 0.0 copy-done.1
  203.7 2.7 multiply_reduce_fusion
  206.4 0.0 copy-start.2
  206.4 1.0 exponential_reduce_fusion
  207.4 0.0 copy-done.2
  207.4 2.7 convolution_convert_fusion.1
  210.2 4.4 %copy.25 = bf16[2048,640]{1,0:T(8,128)(2,1)} copy(bf16[2048,640]{0,1:T(8,128)(2,1)} %bitcast.47) | data formatting | bytes 5242880 | tf_op jit(solution)/shard_map/convert_element_type | solution.py:58
  214.6 0.0 reduce-scatter.5.cloned.1.call-update
  214.6 0.0 reduce-scatter.7.cloned.1.call-start
  214.7 71.8 %reduce-scatter.5.cloned.1.call-done = bf16[128,640]{1,0:T(8,128)(2,1)} async-done(((bf16[2048,640]{1,0:T(8,128)(2,1)}), bf16[128,640]{1,0:T(8,128)(2,1)}) %reduce-scatter.5.cloned.1.call-update) | async-done | bytes 163856 | tf_op jit(solution)/shard_map/reduce_scatter | solution.py:57
  286.4 0.0 copy-done
  286.4 0.0 copy-done.3
  286.4 3.2 convolution_convert_fusion
  289.6 4.3 %copy.28 = bf16[2,128,2560]{1,0,2:T(2,128)(2,1)} copy(bf16[2,128,2560]{2,1,0:T(8,128)(2,1)} %convolution_convert_fusion) | data formatting | bytes 2621440
  293.9 2.6 copy.32
  296.5 0.0 reduce-scatter.7.cloned.1.call-update
  296.5 27.6 %reduce-scatter.7.cloned.1.call-done = bf16[640,256]{1,0:T(8,128)(2,1)} async-done(((bf16[2560,256]{1,0:T(8,128)(2,1)}), bf16[640,256]{1,0:T(8,128)(2,1)}) %reduce-scatter.7.cloned.1.call-update) | async-done | bytes 327696
  324.1 1.8 reshape.30
  325.9 1.9 copy.29
  327.8 1.9 fusion.14
  329.7 2.7 collective-permute-start
  332.4 0.0 copy-done.5
  332.5 12.7 %collective-permute-done = bf16[2,128,640]{2,1,0:T(8,128)(2,1)} collective-permute-done((bf16[2,128,640]{2,1,0:T(8,128)(2,1)}, bf16[2,128,640]{2,1,0:T(8,128)(2,1)}, u32[]{:S(2)}, u32[]{:S(2)}) %collective-permute-start) | collective-permute-done | bytes 327712 | tf_op jit(solution)/shard_map/ppermute | solution.py:13
  345.2 1.7 fusion.17
  (7 shorter events, 0.1 us)
Async XLA Ops:
  6.5 279.9 %copy-start = (bf16[1,2560,640]{2,1,0:T(8,128)(2,1)S(1)}, bf16[1,2560,640]{2,1,0:T(8,128)(2,1)}, u32[]{:S(2)}) copy-start(bf16[1,2560,640]{2,1,0:T(8,128)(2,1)} %param.13) | copy-start | bytes 9830404
  9.8 17.6 %copy-start.4 = (bf16[1,128,640]{2,1,0:T(8,128)(2,1)S(1)}, bf16[1,128,640]{2,1,0:T(8,128)(2,1)}, u32[]{:S(2)}) copy-start(bf16[1,128,640]{2,1,0:T(8,128)(2,1)} %param.11) | copy-start | bytes 491524
  9.8 18.4 %copy-start.6 = (f32[1,2560]{1,0:T(1,128)S(1)}, f32[1,2560]{1,0:T(1,128)}, u32[]{:S(2)}) copy-start(f32[1,2560]{1,0:T(1,128)} %param.15) | copy-start | bytes 30724
  9.8 183.8 %all-to-all-start = ((bf16[16,128,640]{1,2,0:T(8,128)(2,1)}), bf16[16,128,640]{1,2,0:T(8,128)(2,1)}, u32[]{:S(2)}, u32[]{:S(2)}) async-start(bf16[16,128,640]{1,2,0:T(8,128)(2,1)} %stack.24), calls=%async_computation | async-start | bytes 5242880 | tf_op jit(solution)/shard_map/all_to_all | solution.py:44
  25.2 34.5 %all-gather.5.cloned.1.call-start = ((), (), s32[]{:S(2)}) async-start(), calls=%async_computation.4 | async-start | bytes 1638400 | tf_op jit(solution)/shard_map/all_gather | solution.py:33
  25.9 162.6 %all-gather.7.cloned.1.call-start = ((), (), s32[]{:S(2)}) async-start(), calls=%async_computation.5 | async-start | bytes 3481600 | tf_op jit(solution)/shard_map/all_gather | solution.py:35
  26.6 259.8 %reduce-scatter.5.cloned.1.call-start = ((), (), s32[]{:S(2)}) async-start(), calls=%async_computation.3 | async-start | bytes 2785280 | tf_op jit(solution)/shard_map/reduce_scatter | solution.py:57
  198.5 5.2 %copy-start.1 = (bf16[1,128,640]{1,2,0:T(8,128)(2,1)S(1)}, bf16[1,128,640]{1,2,0:T(8,128)(2,1)}, u32[]{:S(2)}) copy-start(bf16[1,128,640]{1,2,0:T(8,128)(2,1)} %copy.20) | copy-start | bytes 491524
  206.4 1.0 copy-start.2
  210.2 76.3 %copy-start.3 = (bf16[1,128,640]{2,1,0:T(8,128)(2,1)S(1)}, bf16[1,128,640]{2,1,0:T(8,128)(2,1)}, u32[]{:S(2)}) copy-start(bf16[1,128,640]{2,1,0:T(8,128)(2,1)} %get-tuple-element.6) | copy-start | bytes 491524
  214.6 109.5 %reduce-scatter.7.cloned.1.call-start = ((), (), s32[]{:S(2)}) async-start(), calls=%async_computation.6 | async-start | bytes 1638400
  293.9 38.5 %copy-start.5 = (bf16[128,640]{1,0:T(8,128)(2,1)S(1)}, bf16[128,640]{1,0:T(8,128)(2,1)}, u32[]{:S(2)}) copy-start(bf16[128,640]{1,0:T(8,128)(2,1)} %param.10) | copy-start | bytes 491524
  329.7 15.5 %collective-permute-start = (bf16[2,128,640]{2,1,0:T(8,128)(2,1)}, bf16[2,128,640]{2,1,0:T(8,128)(2,1)}, u32[]{:S(2)}, u32[]{:S(2)}) collective-permute-start(bf16[2,128,640]{2,1,0:T(8,128)(2,1)} %fusion.14), channel_id=1, source_target_pairs={{64,0},{128,64},{192,128},{256,192},{320,256},{384,320},{448,384},... | collective-permute-start | bytes 983048 | tf_op jit(solution)/shard_map/ppermute | solution.py:13
Sparse Core Ops, SparseCore 0:
  28.1 31.4 all-gather.4
  61.7 126.7 all-gather.6
  214.7 71.6 reduce-scatter.4
  296.7 27.3 reduce-scatter.6
